TPU v7x, 128 devices: a whole 4x4x4 slice. The times are simulated.
128 devices in a mesh: req: 16 (over x, z), mlp: 8 (over y, core).
Axes of the slice: x: 4, y: 4, z: 4, core: 2. Of those that a mesh axis runs over, the one named last changes fastest.
Arguments:
- patches: bfloat16 [15360, 4096], P('req'), may hold values from -6 to 6
- norm_gain: float32 [4096], replicated, may hold values from 0.25 to 1.75
- norm_bias: float32 [4096], replicated, may hold values from -3 to 3
- gate_weight: bfloat16 [4096, 8192], P(None, ('req', 'mlp')), may hold values from -0.09375 to 0.09375
- up_weight: bfloat16 [4096, 8192], P(None, ('req', 'mlp')), may hold values from -0.09375 to 0.09375
- down_weight: bfloat16 [4096, 8192], P(None, ('req', 'mlp')), may hold values from -0.0625 to 0.0625
- layer_scale: float32 [4096], replicated, may hold values from 0.25 to 2.5
- projection: bfloat16 [4, 4096, 4096], P(None, 'mlp', 'req'), may hold values from -0.046875 to 0.046875
- text_rows: bfloat16 [65536, 4096], P(('req', 'mlp')), may hold values from -6 to 6
- destination: int32 [3840], replicated, may hold values from -1 to 65535, as said below
Outputs:
- patch_out: bfloat16 [15360, 4096], P('req', 'mlp')
- streams: bfloat16 [65536, 4096], P(('req', 'mlp'))
Inputs may be any that keep to these rules, and one draw needn't show every extreme that they name: `destination`: values other than -1 are distinct positions; the positions landing in one piece of 512 consecutive positions (a stream holds 8 pieces) form one run of consecutive positions, at least one and at most 30 of them, and some piece receives exactly 30.
All inputs are finite; a program needn't handle non-finite values.
Results may differ from a plain program's by a relative error of at most 0.015.
Values may be sent and summed in bfloat16 or wider, within the bound.
No kernel may reach another device: no remote copies, remote signals or barrier semaphores. Data moves between devices by JAX's collectives and lax.ppermute only.
A program may use at most 128 MiB of HBM per device.

v0:
```python
import jax
import jax.numpy as jnp
from jax import lax
from jax.sharding import PartitionSpec as P


def layer_norm(values, norm_gain, norm_bias):
    row_mean = jnp.mean(values, axis=-1, keepdims=True)
    centred = values - row_mean
    variance = jnp.mean(centred * centred, axis=-1, keepdims=True)
    return centred * lax.rsqrt(variance + 1e-06) * norm_gain + norm_bias


def shards(
    patches,
    norm_gain,
    norm_bias,
    gate_weight,
    up_weight,
    down_weight,
    layer_scale,
    projection,
    text_rows,
    destination,
):
    req_count = lax.axis_size("req")
    mlp_count = lax.axis_size("mlp")
    req_index = lax.axis_index("req")
    mlp_index = lax.axis_index("mlp")
    rows_here, model_width = patches.shape
    feat_width = model_width // mlp_count
    inputs = patches.astype(jnp.float32)
    normed = layer_norm(inputs, norm_gain, norm_bias).astype(jnp.bfloat16)
    gate_act = jnp.dot(
        normed,
        lax.all_gather(gate_weight, "req", axis=1, tiled=True),
        preferred_element_type=jnp.float32,
    )
    up_act = jnp.dot(
        normed,
        lax.all_gather(up_weight, "req", axis=1, tiled=True),
        preferred_element_type=jnp.float32,
    )
    hidden = (jax.nn.silu(gate_act) * up_act).astype(jnp.bfloat16)
    ffn_local = lax.dot_general(
        hidden,
        lax.all_gather(down_weight, "req", axis=1, tiled=True),
        (((1,), (1,)), ((), ())),
        preferred_element_type=jnp.float32,
    )
    partial_value = lax.optimization_barrier(ffn_local.astype(jnp.bfloat16)).astype(jnp.float32)
    ffn_feats = lax.psum_scatter(
        partial_value.astype(jnp.bfloat16), "mlp", scatter_dimension=1, tiled=True
    ).astype(jnp.float32)
    scale_here = lax.dynamic_slice_in_dim(layer_scale, mlp_index * feat_width, feat_width)
    own_inputs = lax.dynamic_slice_in_dim(inputs, mlp_index * feat_width, feat_width, axis=1)
    patch_out = (own_inputs + scale_here * ffn_feats).astype(jnp.bfloat16)
    merged = patch_out.reshape(rows_here // 4, 4 * feat_width)
    weight_cols = projection.reshape(4 * feat_width, projection.shape[2])
    piece_rows = text_rows.shape[0]
    slot_count = destination.shape[0]
    bucket_count = req_count * mlp_count
    capacity = slot_count // bucket_count
    is_valid = destination >= 0
    piece_ids = jnp.where(is_valid, destination // piece_rows, -1)
    offsets = destination % piece_rows
    bucket_hit = piece_ids[:, None] == jnp.arange(bucket_count, dtype=jnp.int32)[None, :]
    first_off = jnp.min(jnp.where(bucket_hit, offsets[:, None], piece_rows), axis=0)
    counts = jnp.sum(bucket_hit.astype(jnp.int32), axis=0)
    slot_first = jnp.sum(jnp.where(bucket_hit, first_off[None, :], 0), axis=1)
    slot_rank = offsets - slot_first
    stream_ids = piece_ids // mlp_count
    piece_in = piece_ids % mlp_count
    rows_at = piece_in * (req_count * capacity) + stream_ids * capacity + slot_rank
    rows_at = jnp.where(is_valid, rows_at, bucket_count * capacity)
    sources = (
        jnp.full((bucket_count * capacity,), -1, jnp.int32)
        .at[rows_at]
        .set(jnp.arange(slot_count, dtype=jnp.int32), mode="drop")
    )
    every_row = lax.all_gather(merged, "req", axis=0, tiled=True)
    picked_rows = jnp.take(every_row, jnp.maximum(sources, 0), axis=0)
    picked_rows = jnp.where(sources[:, None] >= 0, picked_rows, jnp.zeros_like(picked_rows))
    summed = lax.psum_scatter(
        jnp.dot(picked_rows, weight_cols, preferred_element_type=jnp.float32).astype(jnp.bfloat16),
        "mlp",
        scatter_dimension=0,
        tiled=True,
    )
    arrived = lax.all_to_all(summed, "req", split_axis=0, concat_axis=1, tiled=True)
    bucket_here = req_index * mlp_count + mlp_index
    start_here = first_off[bucket_here]
    count_here = counts[bucket_here]
    positions = jnp.arange(piece_rows, dtype=jnp.int32) - start_here
    inside = (positions >= 0) & (positions < count_here)
    image_rows = jnp.take(arrived, jnp.clip(positions, 0, capacity - 1), axis=0)
    streams = jnp.where(inside[:, None], image_rows, text_rows)
    return (patch_out, streams)


def solution(mesh):
    return jax.shard_map(
        shards,
        mesh=mesh,
        in_specs=(
            P("req", None),
            P(),
            P(),
            P(None, ("req", "mlp")),
            P(None, ("req", "mlp")),
            P(None, ("req", "mlp")),
            P(),
            P(None, "mlp", "req"),
            P(("req", "mlp"), None),
            P(),
        ),
        out_specs=(P("req", "mlp"), P(("req", "mlp"), None)),
        check_vma=False,
    )
```

profile of v0, /device:TPU:0, one launch (start us, length us, event | category | flops | bytes accessed | tf_op | source)
XLA Modules:
  0.0 527.9 jit_solution(9855831558795438825)
XLA Ops:
  7.2 0.7 all-gather.5.cloned.1.call-update
  8.0 0.7 all-gather.7.cloned.1.call-update
  8.7 0.7 all-gather.9.cloned.1.call-update
  9.5 4.5 convert_reduce_fusion
  14.0 1.0 copy-done.1
  14.9 2.2 multiply_reduce_fusion
  17.1 66.4 %all-gather.5.cloned.1.call-done = bf16[4096,1024]{0,1:T(8,128)(2,1)} async-done(((bf16[4096,64]{0,1:T(8,128)(2,1)}), bf16[4096,1024]{0,1:T(8,128)(2,1)}) %all-gather.5.cloned.1.call-update) | async-done | bytes 8388624 | tf_op jit(solution)/shard_map/all_gather | solution.py:36
  83.5 14.4 %fusion.31 = f32[960,1024]{1,0:T(8,128)} fusion(bf16[4096,1024]{0,1:T(8,128)(2,1)} %all-gather.5.cloned.1.call-done, bf16[960,4096]{1,0:T(8,128)(2,1)} %param.10, f32[4096]{0:T(1024)S(1)} %copy-done.4, f32[4096]{0:T(1024)S(1)} %copy-done.5, f32[960]{0:T(1024)S(1)} %add_rsqrt_fusion, f32[960]{0:T(1024)S(1)} %broadcast_multiply_fusion), kind=kOutput, calls=%fused_computation.68 | convolution fusion | flops 8076656640 | bytes 20225536 | tf_op jit(solution)/shard_map/dot_general | solution.py:34
  97.9 58.2 %all-gather.7.cloned.1.call-done = bf16[4096,1024]{0,1:T(8,128)(2,1)} async-done(((bf16[4096,64]{0,1:T(8,128)(2,1)}), bf16[4096,1024]{0,1:T(8,128)(2,1)}) %all-gather.7.cloned.1.call-update) | async-done | bytes 8388624 | tf_op jit(solution)/shard_map/all_gather | solution.py:41
  156.1 72.6 %all-gather.9.cloned.1.call-done = bf16[4096,1024]{0,1:T(8,128)(2,1)} async-done(((bf16[4096,64]{0,1:T(8,128)(2,1)}), bf16[4096,1024]{0,1:T(8,128)(2,1)}) %all-gather.9.cloned.1.call-update) | async-done | bytes 8388624 | tf_op jit(solution)/shard_map/all_gather | solution.py:47
  228.7 25.9 %convolution_convert_fusion = bf16[960,4096]{1,0:T(8,128)(2,1)} fusion(bf16[4096,1024]{0,1:T(8,128)(2,1)} %all-gather.9.cloned.1.call-done, f32[960,1024]{1,0:T(8,128)} %fusion.31, bf16[4096,1024]{0,1:T(8,128)(2,1)} %all-gather.7.cloned.1.call-done, bf16[960,4096]{1,0:T(8,128)(2,1)} %param.10, f32[4096]{0:T(1024)S(1)} %copy-done.4, f32[4096]{0:T(1024)S(1)} %copy-done.5, ...), kind=kOutput, calls=%fused_computation.13 | convolution fusion | flops 16139550720 | bytes 36478464 | tf_op jit(solution)/shard_map/dot_general | solution.py:45
  254.7 11.3 %convert_element_type.26 = f32[960,4096]{1,0:T(8,128)} convert(bf16[960,4096]{1,0:T(8,128)(2,1)} %param.10) | non-fusion elementwise | flops 3932160 | bytes 23592960 | tf_op jit(solution)/shard_map/convert_element_type | solution.py:32
  266.0 0.8 dynamic_slice.13
  266.7 37.6 %reduce-scatter.3.cloned.1.call-done = bf16[960,512]{1,0:T(8,128)(2,1)} async-done(((bf16[960,4096]{1,0:T(8,128)(2,1)}), bf16[960,512]{1,0:T(8,128)(2,1)}) %reduce-scatter.3.cloned.1.call-update) | async-done | bytes 983056 | tf_op jit(solution)/shard_map/reduce_scatter | solution.py:52
  304.3 2.2 add_convert_fusion.1
  306.5 1.5 reshape.67
  308.1 2.5 select_reduce_fusion.1
  310.6 2.4 convert_reduce_fusion.1
  313.1 14.6 %scatter_custom_fusion = s32[3840]{0:T(1024)S(1)} fusion(s32[3840]{0:T(1024)S(1)} %compare_select_fusion, s32[3840]{0:T(1024)S(1)} %iota.16, s32[]{:T(128)} %constant.104.clone.1), kind=kCustom, calls=%fused_computation.51 | custom fusion | bytes 15364 | tf_op jit(solution)/shard_map/scatter | solution.py:79
  327.7 86.2 %all-gather.11.cloned.1.call-done = bf16[3840,2048]{1,0:T(8,128)(2,1)} async-done(((bf16[240,2048]{1,0:T(8,128)(2,1)}), bf16[3840,2048]{1,0:T(8,128)(2,1)}) %all-gather.11.cloned.1.call-update) | async-done | bytes 15728656 | tf_op jit(solution)/shard_map/all_gather | solution.py:81
  413.9 37.0 %gather_fusion = bf16[3840,2048]{1,0:T(8,128)(2,1)} fusion(bf16[3840,2048]{1,0:T(8,128)(2,1)} %all-gather.11.cloned.1.call-done, s32[4096]{0:T(1024)S(1)} %pad_clamp_fusion), kind=kCustom, calls=%fused_computation | custom fusion | bytes 31472640 | tf_op jit(solution)/shard_map/jit(_take)/gather | solution.py:82
  450.9 9.9 %fusion.7 = bf16[3840,256]{1,0:T(8,128)(2,1)} fusion(bf16[2048,256]{1,0:T(8,128)(2,1)S(1)} %bitcast.13, bf16[3840,2048]{1,0:T(8,128)(2,1)} %gather_fusion, pred[3840]{0:T(1024)(128)(4,1)S(1)} %get-tuple-element.5, pred[3840]{0:T(1024)(128)(4,1)S(1)} %get-tuple-element.4), kind=kOutput, calls=%fused_computation.14 | convolution fusion | flops 4043243520 | bytes 18750976 | tf_op jit(solution)/shard_map/dot_general | solution.py:85
  460.8 0.6 dynamic_slice.14
  461.4 0.6 dynamic_slice.15
  462.1 31.9 %reduce-scatter.5.cloned.1.call-done = bf16[480,256]{1,0:T(8,128)(2,1)} async-done(((bf16[3840,256]{1,0:T(8,128)(2,1)}), bf16[480,256]{1,0:T(8,128)(2,1)}) %reduce-scatter.5.cloned.1.call-update) | async-done | bytes 245776 | tf_op jit(solution)/shard_map/reduce_scatter | solution.py:84
  494.0 1.7 all_to_all.14
  495.7 6.9 %all-to-all-start = ((bf16[16,30,256]{2,1,0:T(8,128)(2,1)}), bf16[16,30,256]{2,1,0:T(8,128)(2,1)S(1)}, u32[]{:S(2)}, u32[]{:S(2)}) async-start(bf16[16,30,256]{2,1,0:T(8,128)(2,1)} %all_to_all.14), calls=%async_computation.2 | async-start | bytes 524288 | tf_op jit(solution)/shard_map/all_to_all | solution.py:90
  502.6 1.3 fusion.27
  503.9 0.6 compare_select_fusion.1
  504.6 6.5 %all-to-all-done = bf16[16,30,256]{2,1,0:T(8,128)(2,1)S(1)} async-done(((bf16[16,30,256]{2,1,0:T(8,128)(2,1)}), bf16[16,30,256]{2,1,0:T(8,128)(2,1)S(1)}, u32[]{:S(2)}, u32[]{:S(2)}) %all-to-all-start) | async-done | bytes 245792 | tf_op jit(solution)/shard_map/all_to_all | solution.py:90
  511.4 4.4 gather_fusion.1
  515.7 5.3 select_select_fusion
  (32 shorter events, 0.7 us)
Async XLA Ops:
  7.2 443.7 %copy-start = (bf16[4,512,256]{2,1,0:T(8,128)(2,1)S(1)}, bf16[4,512,256]{2,1,0:T(8,128)(2,1)}, u32[]{:S(2)}) copy-start(bf16[4,512,256]{2,1,0:T(8,128)(2,1)} %param.17) | copy-start | bytes 3145732
  7.2 76.3 %all-gather.5.cloned.1.call-start = ((), (), s32[]{:S(2)}) async-start(), calls=%async_computation.3 | async-start | bytes 8912896 | tf_op jit(solution)/shard_map/all_gather | solution.py:36
  7.9 148.2 %all-gather.7.cloned.1.call-start = ((), (), s32[]{:S(2)}) async-start(), calls=%async_computation.4 | async-start | bytes 8912896 | tf_op jit(solution)/shard_map/all_gather | solution.py:41
  8.7 220.1 %all-gather.9.cloned.1.call-start = ((), (), s32[]{:S(2)}) async-start(), calls=%async_computation.5 | async-start | bytes 8912896 | tf_op jit(solution)/shard_map/all_gather | solution.py:47
  9.4 294.9 %reduce-scatter.3.cloned.1.call-start = ((), (), s32[]{:S(2)}) async-start(), calls=%async_computation.6 | async-start | bytes 8847360 | tf_op jit(solution)/shard_map/reduce_scatter | solution.py:52
  9.4 5.5 %copy-start.1 = (bf16[960,4096]{1,0:T(8,128)(2,1)S(1)}, bf16[960,4096]{1,0:T(8,128)(2,1)}, u32[]{:S(2)}) copy-start(bf16[960,4096]{1,0:T(8,128)(2,1)} %param.10) | copy-start | bytes 23592964
  9.5 74.1 %copy-start.4 = (f32[4096]{0:T(1024)S(1)}, f32[4096]{0:T(1024)}, u32[]{:S(2)}) copy-start(f32[4096]{0:T(1024)} %param.12) | copy-start | bytes 49156
  9.5 74.1 %copy-start.5 = (f32[4096]{0:T(1024)S(1)}, f32[4096]{0:T(1024)}, u32[]{:S(2)}) copy-start(f32[4096]{0:T(1024)} %param.11) | copy-start | bytes 49156
  254.6 159.3 %all-gather.11.cloned.1.call-start = ((), (), s32[]{:S(2)}) async-start(), calls=%async_computation.7 | async-start | bytes 16711680 | tf_op jit(solution)/shard_map/all_gather | solution.py:81
  254.7 53.4 %copy-start.3 = (s32[3840]{0:T(1024)S(1)}, s32[3840]{0:T(1024)}, u32[]{:S(2)}) copy-start(s32[3840]{0:T(1024)} %param.19) | copy-start | bytes 46084
  306.5 144.4 %copy-start.2 = (bf16[960,512]{1,0:T(8,128)(2,1)}, bf16[960,512]{1,0:T(8,128)(2,1)S(1)}, u32[]{:S(2)}) copy-start(bf16[960,512]{1,0:T(8,128)(2,1)S(1)} %add_convert_fusion.1) | copy-start | bytes 2949124
  308.0 186.0 %reduce-scatter.5.cloned.1.call-start = ((), (), s32[]{:S(2)}) async-start(), calls=%async_computation.8 | async-start | bytes 2211840 | tf_op jit(solution)/shard_map/reduce_scatter | solution.py:84
  495.7 15.4 %all-to-all-start = ((bf16[16,30,256]{2,1,0:T(8,128)(2,1)}), bf16[16,30,256]{2,1,0:T(8,128)(2,1)S(1)}, u32[]{:S(2)}, u32[]{:S(2)}) async-start(bf16[16,30,256]{2,1,0:T(8,128)(2,1)} %all_to_all.14), calls=%async_computation.2 | async-start | bytes 524288 | tf_op jit(solution)/shard_map/all_to_all | solution.py:90
Sparse Core Ops, SparseCore 0:
  10.2 73.3 all-gather.4
  85.7 70.4 all-gather.6
  158.3 70.4 all-gather.8
  254.7 49.5 reduce-scatter.2
  308.2 105.6 all-gather.10
  460.9 33.0 reduce-scatter.4
where the time goes:
time: 528 us
  waiting for transfers between devices  362 us (69%)
  local copies, waits for them, and re-layouts  62.5 us (12%)
  matrix products  50.1 us (9%)
  other arithmetic  32.3 us (6%)
  between operations  14.3 us (3%)
  starting transfers between devices  7.14 us (1%)
    all_gather x1, waiting for transfers between devices, shards(): every_row = lax.all_gather(merged, 'req', axis=0, tiled=True)  86.2 us
    all_gather x1, waiting for transfers between devices, shards(): lax.all_gather(down_weight, 'req', axis=1, tiled=True)  72.6 us
    all_gather x1, waiting for transfers between devices, shards(): lax.all_gather(gate_weight, 'req', axis=1, tiled=True)  66.4 us
    all_gather x1, waiting for transfers between devices, shards(): lax.all_gather(up_weight, 'req', axis=1, tiled=True)  58.2 us
    reduce_scatter x1, waiting for transfers between devices, shards(): lax.psum_scatter(partial_value.astype(jnp.bfloat16), 'mlp', scatter_dimen...  37.6 us
    gather x1, local copies, waits for them, and re-layouts, shards(): picked_rows = jnp.take(every_row, jnp.maximum(sources, 0), axis=0)  37 us
    reduce_scatter x1, waiting for transfers between devices, shards(): lax.psum_scatter(jnp.dot(picked_rows, weight_cols, preferred_element_type...  31.9 us
    dot_general x1, matrix products, shards(): lax.dot_general(hidden, lax.all_gather(down_weight, 'req', axis=1, tiled=...  25.9 us
  transfers between devices with their start and end apart: 7, of which 7 were waited for; matrix products, arithmetic and copies ran while one was open for 11% of the time, Pallas kernels for 0%

commit v1 on v0

--- a/solution.py
+++ b/solution.py
@@ -2,6 +2,13 @@
 import jax.numpy as jnp
 from jax import lax
 from jax.sharding import PartitionSpec as P
+
+
+def gather_over(x, mesh_axis, d):
+    size = lax.axis_size(mesh_axis)
+    pieces = jnp.stack([x for _ in range(size)])
+    pieces = lax.all_to_all(pieces, mesh_axis, split_axis=0, concat_axis=0)
+    return jnp.concatenate(pieces, axis=d)
 
 
 def layer_norm(values, norm_gain, norm_bias):
@@ -32,9 +39,7 @@
     inputs = patches.astype(jnp.float32)
     normed = layer_norm(inputs, norm_gain, norm_bias).astype(jnp.bfloat16)
     gate_act = jnp.dot(
-        normed,
-        lax.all_gather(gate_weight, "req", axis=1, tiled=True),
-        preferred_element_type=jnp.float32,
+        normed, gather_over(gate_weight, "req", 1), preferred_element_type=jnp.float32
     )
     up_act = jnp.dot(
         normed,

time: 528 us -> 570 us (1.080)
  waiting for transfers between devices: 362 us -> 387 us
  starting transfers between devices: 7.14 us -> 15.2 us
    all_to_all x0 -> x1, waiting for transfers between devices: none -> 143 us  [gather_over(): pieces = lax.all_to_all(pieces, mesh_axis, split_axis=0, concat_axis=0)]
    all_gather x1 -> x0, waiting for transfers between devices: 66.4 us -> none  [shards(): lax.all_gather(gate_weight, 'req', axis=1, tiled=True)]
    all_gather x1, waiting for transfers between devices: 58.2 us -> 5.99 us  [shards(): lax.all_gather(up_weight, 'req', axis=1, tiled=True)]
    all_to_all x0 -> x1, starting transfers between devices: none -> 8.01 us  [gather_over(): pieces = lax.all_to_all(pieces, mesh_axis, split_axis=0, concat_axis=0)]
where the time goes in v1:
time: 570 us; the launch traced here: 569 us
  waiting for transfers between devices  387 us (68%)
  local copies, waits for them, and re-layouts  66.7 us (12%)
  matrix products  50.4 us (9%)
  other arithmetic  35.6 us (6%)
  starting transfers between devices  15.2 us (3%)
  between operations  14 us (2%)
    all_to_all x1, waiting for transfers between devices, gather_over(): pieces = lax.all_to_all(pieces, mesh_axis, split_axis=0, concat_axis=0)  143 us
    all_gather x1, waiting for transfers between devices, shards(): every_row = lax.all_gather(merged, 'req', axis=0, tiled=True)  86.2 us
    all_gather x1, waiting for transfers between devices, shards(): lax.all_gather(down_weight, 'req', axis=1, tiled=True)  74.8 us
    reduce_scatter x1, waiting for transfers between devices, shards(): lax.psum_scatter(partial_value.astype(jnp.bfloat16), 'mlp', scatter_dimen...  37.6 us
    gather x1, local copies, waits for them, and re-layouts, shards(): picked_rows = jnp.take(every_row, jnp.maximum(sources, 0), axis=0)  37 us
    reduce_scatter x1, waiting for transfers between devices, shards(): lax.psum_scatter(jnp.dot(picked_rows, weight_cols, preferred_element_type...  31.9 us
    dot_general x1, matrix products, shards(): lax.dot_general(hidden, lax.all_gather(down_weight, 'req', axis=1, tiled=...  25.9 us
    scatter x1, local copies, waits for them, and re-layouts, shards(): sources = jnp.full((bucket_count * capacity,), -1, jnp.int32).at[rows_at]...  14.6 us
  transfers between devices with their start and end apart: 7, of which 7 were waited for; matrix products, arithmetic and copies ran while one was open for 11% of the time, Pallas kernels for 0%

profile of v1, /device:TPU:0, one launch (start us, length us, event | category | flops | bytes accessed | tf_op | source)
XLA Modules:
  0.0 568.9 jit_solution(251003677645856364)
XLA Ops:
  7.2 0.7 all-gather.4.cloned.1.call-update
  8.0 0.7 all-gather.6.cloned.1.call-update
  8.7 5.3 stack.2
  14.0 8.0 %all-to-all-start = ((bf16[16,4096,64]{1,2,0:T(8,128)(2,1)}), bf16[16,4096,64]{1,2,0:T(8,128)(2,1)}, u32[]{:S(2)}, u32[]{:S(2)}) async-start(bf16[16,4096,64]{1,2,0:T(8,128)(2,1)} %stack.2), calls=%async_computation | async-start | bytes 16777216 | tf_op jit(solution)/shard_map/all_to_all | solution.py:10
  22.1 4.6 convert_reduce_fusion
  26.7 5.4 multiply_reduce_fusion
  32.2 142.6 %all-to-all-done = bf16[16,4096,64]{1,2,0:T(8,128)(2,1)} async-done(((bf16[16,4096,64]{1,2,0:T(8,128)(2,1)}), bf16[16,4096,64]{1,2,0:T(8,128)(2,1)}, u32[]{:S(2)}, u32[]{:S(2)}) %all-to-all-start) | async-done | bytes 8388640 | tf_op jit(solution)/shard_map/all_to_all | solution.py:10
  174.7 14.6 %fusion.31 = f32[960,1024]{1,0:T(8,128)} fusion(bf16[4096,1024]{0,1:T(8,128)(2,1)} %bitcast.1, bf16[960,4096]{1,0:T(8,128)(2,1)} %param.10, f32[4096]{0:T(1024)S(1)} %copy-done.3, f32[4096]{0:T(1024)S(1)} %copy-done.4, f32[960]{0:T(1024)S(1)} %add_rsqrt_fusion, f32[960]{0:T(1024)S(1)} %broadcast_multiply_fusion), kind=kOutput, calls=%fused_computation.68 | convolution fusion | flops 8076656640 | bytes 20225536 | tf_op jit(solution)/shard_map/dot_general | solution.py:41
  189.3 6.0 %all-gather.4.cloned.1.call-done = bf16[4096,1024]{0,1:T(8,128)(2,1)} async-done(((bf16[4096,64]{0,1:T(8,128)(2,1)}), bf16[4096,1024]{0,1:T(8,128)(2,1)}) %all-gather.4.cloned.1.call-update) | async-done | bytes 8388624 | tf_op jit(solution)/shard_map/all_gather | solution.py:46
  195.3 74.8 %all-gather.6.cloned.1.call-done = bf16[4096,1024]{0,1:T(8,128)(2,1)} async-done(((bf16[4096,64]{0,1:T(8,128)(2,1)}), bf16[4096,1024]{0,1:T(8,128)(2,1)}) %all-gather.6.cloned.1.call-update) | async-done | bytes 8388624 | tf_op jit(solution)/shard_map/all_gather | solution.py:52
  270.1 25.9 %convolution_convert_fusion = bf16[960,4096]{1,0:T(8,128)(2,1)} fusion(bf16[4096,1024]{0,1:T(8,128)(2,1)} %all-gather.6.cloned.1.call-done, f32[960,1024]{1,0:T(8,128)} %fusion.31, bf16[4096,1024]{0,1:T(8,128)(2,1)} %all-gather.4.cloned.1.call-done, bf16[960,4096]{1,0:T(8,128)(2,1)} %param.10, f32[4096]{0:T(1024)S(1)} %copy-done.3, f32[4096]{0:T(1024)S(1)} %copy-done.4, ...), kind=kOutput, calls=%fused_computation.13 | convolution fusion | flops 16139550720 | bytes 36478464 | tf_op jit(solution)/shard_map/dot_general | solution.py:50
  296.0 11.3 %convert_element_type.26 = f32[960,4096]{1,0:T(8,128)} convert(bf16[960,4096]{1,0:T(8,128)(2,1)} %param.10) | non-fusion elementwise | flops 3932160 | bytes 23592960 | tf_op jit(solution)/shard_map/convert_element_type | solution.py:39
  307.3 0.8 dynamic_slice.13
  308.1 37.6 %reduce-scatter.3.cloned.1.call-done = bf16[960,512]{1,0:T(8,128)(2,1)} async-done(((bf16[960,4096]{1,0:T(8,128)(2,1)}), bf16[960,512]{1,0:T(8,128)(2,1)}) %reduce-scatter.3.cloned.1.call-update) | async-done | bytes 983056 | tf_op jit(solution)/shard_map/reduce_scatter | solution.py:57
  345.7 2.2 add_convert_fusion.1
  347.8 1.5 reshape.77
  349.5 2.5 select_reduce_fusion.1
  352.0 2.4 convert_reduce_fusion.1
  354.4 14.6 %scatter_custom_fusion = s32[3840]{0:T(1024)S(1)} fusion(s32[3840]{0:T(1024)S(1)} %compare_select_fusion, s32[3840]{0:T(1024)S(1)} %iota.16, s32[]{:T(128)} %constant.104.clone.1), kind=kCustom, calls=%fused_computation.51 | custom fusion | bytes 15364 | tf_op jit(solution)/shard_map/scatter | solution.py:84
  369.1 86.2 %all-gather.8.cloned.1.call-done = bf16[3840,2048]{1,0:T(8,128)(2,1)} async-done(((bf16[240,2048]{1,0:T(8,128)(2,1)}), bf16[3840,2048]{1,0:T(8,128)(2,1)}) %all-gather.8.cloned.1.call-update) | async-done | bytes 15728656 | tf_op jit(solution)/shard_map/all_gather | solution.py:86
  455.3 37.0 %gather_fusion = bf16[3840,2048]{1,0:T(8,128)(2,1)} fusion(bf16[3840,2048]{1,0:T(8,128)(2,1)} %all-gather.8.cloned.1.call-done, s32[4096]{0:T(1024)S(1)} %pad_clamp_fusion), kind=kCustom, calls=%fused_computation | custom fusion | bytes 31472640 | tf_op jit(solution)/shard_map/jit(_take)/gather | solution.py:87
  492.2 9.9 %fusion.7 = bf16[3840,256]{1,0:T(8,128)(2,1)} fusion(bf16[2048,256]{1,0:T(8,128)(2,1)S(1)} %bitcast.15, bf16[3840,2048]{1,0:T(8,128)(2,1)} %gather_fusion, pred[3840]{0:T(1024)(128)(4,1)S(1)} %get-tuple-element.5, pred[3840]{0:T(1024)(128)(4,1)S(1)} %get-tuple-element.4), kind=kOutput, calls=%fused_computation.14 | convolution fusion | flops 4043243520 | bytes 18750976 | tf_op jit(solution)/shard_map/dot_general | solution.py:90
  502.2 0.6 dynamic_slice.14
  502.8 0.6 dynamic_slice.15
  503.4 31.9 %reduce-scatter.5.cloned.1.call-done = bf16[480,256]{1,0:T(8,128)(2,1)} async-done(((bf16[3840,256]{1,0:T(8,128)(2,1)}), bf16[480,256]{1,0:T(8,128)(2,1)}) %reduce-scatter.5.cloned.1.call-update) | async-done | bytes 245776 | tf_op jit(solution)/shard_map/reduce_scatter | solution.py:89
  535.3 1.7 all_to_all.18
  537.0 7.0 %all-to-all-start.1 = ((bf16[16,30,256]{2,1,0:T(8,128)(2,1)}), bf16[16,30,256]{2,1,0:T(8,128)(2,1)S(1)}, u32[]{:S(2)}, u32[]{:S(2)}) async-start(bf16[16,30,256]{2,1,0:T(8,128)(2,1)} %all_to_all.18), calls=%async_computation.3 | async-start | bytes 524288 | tf_op jit(solution)/shard_map/all_to_all | solution.py:95
  544.0 1.2 fusion.27
  545.2 0.6 compare_select_fusion.1
  545.8 6.7 %all-to-all-done.1 = bf16[16,30,256]{2,1,0:T(8,128)(2,1)S(1)} async-done(((bf16[16,30,256]{2,1,0:T(8,128)(2,1)}), bf16[16,30,256]{2,1,0:T(8,128)(2,1)S(1)}, u32[]{:S(2)}, u32[]{:S(2)}) %all-to-all-start.1) | async-done | bytes 245792 | tf_op jit(solution)/shard_map/all_to_all | solution.py:95
  552.7 4.4 gather_fusion.1
  557.1 5.3 select_select_fusion
  (30 shorter events, 0.6 us)
Async XLA Ops:
  7.2 485.1 %copy-start = (bf16[4,512,256]{2,1,0:T(8,128)(2,1)S(1)}, bf16[4,512,256]{2,1,0:T(8,128)(2,1)}, u32[]{:S(2)}) copy-start(bf16[4,512,256]{2,1,0:T(8,128)(2,1)} %param.17) | copy-start | bytes 3145732
  7.2 188.1 %all-gather.4.cloned.1.call-start = ((), (), s32[]{:S(2)}) async-start(), calls=%async_computation.4 | async-start | bytes 8912896 | tf_op jit(solution)/shard_map/all_gather | solution.py:46
  7.9 262.2 %all-gather.6.cloned.1.call-start = ((), (), s32[]{:S(2)}) async-start(), calls=%async_computation.5 | async-start | bytes 8912896 | tf_op jit(solution)/shard_map/all_gather | solution.py:52
  14.0 160.7 %all-to-all-start = ((bf16[16,4096,64]{1,2,0:T(8,128)(2,1)}), bf16[16,4096,64]{1,2,0:T(8,128)(2,1)}, u32[]{:S(2)}, u32[]{:S(2)}) async-start(bf16[16,4096,64]{1,2,0:T(8,128)(2,1)} %stack.2), calls=%async_computation | async-start | bytes 16777216 | tf_op jit(solution)/shard_map/all_to_all | solution.py:10
  22.0 152.7 %copy-start.3 = (f32[4096]{0:T(1024)S(1)}, f32[4096]{0:T(1024)}, u32[]{:S(2)}) copy-start(f32[4096]{0:T(1024)} %param.12) | copy-start | bytes 49156
  22.0 152.7 %copy-start.4 = (f32[4096]{0:T(1024)S(1)}, f32[4096]{0:T(1024)}, u32[]{:S(2)}) copy-start(f32[4096]{0:T(1024)} %param.11) | copy-start | bytes 49156
  22.0 323.6 %reduce-scatter.3.cloned.1.call-start = ((), (), s32[]{:S(2)}) async-start(), calls=%async_computation.6 | async-start | bytes 8847360 | tf_op jit(solution)/shard_map/reduce_scatter | solution.py:57
  296.0 159.3 %all-gather.8.cloned.1.call-start = ((), (), s32[]{:S(2)}) async-start(), calls=%async_computation.7 | async-start | bytes 16711680 | tf_op jit(solution)/shard_map/all_gather | solution.py:86
  296.0 53.4 %copy-start.2 = (s32[3840]{0:T(1024)S(1)}, s32[3840]{0:T(1024)}, u32[]{:S(2)}) copy-start(s32[3840]{0:T(1024)} %param.19) | copy-start | bytes 46084
  347.8 144.4 %copy-start.1 = (bf16[960,512]{1,0:T(8,128)(2,1)}, bf16[960,512]{1,0:T(8,128)(2,1)S(1)}, u32[]{:S(2)}) copy-start(bf16[960,512]{1,0:T(8,128)(2,1)S(1)} %add_convert_fusion.1) | copy-start | bytes 2949124
  349.4 185.9 %reduce-scatter.5.cloned.1.call-start = ((), (), s32[]{:S(2)}) async-start(), calls=%async_computation.8 | async-start | bytes 2211840 | tf_op jit(solution)/shard_map/reduce_scatter | solution.py:89
  537.0 15.5 %all-to-all-start.1 = ((bf16[16,30,256]{2,1,0:T(8,128)(2,1)}), bf16[16,30,256]{2,1,0:T(8,128)(2,1)S(1)}, u32[]{:S(2)}, u32[]{:S(2)}) async-start(bf16[16,30,256]{2,1,0:T(8,128)(2,1)} %all_to_all.18), calls=%async_computation.3 | async-start | bytes 524288 | tf_op jit(solution)/shard_map/all_to_all | solution.py:95
Sparse Core Ops, SparseCore 0:
  10.2 185.1 all-gather.3
  197.5 72.5 all-gather.5
  296.1 49.5 reduce-scatter.2
  349.5 105.6 all-gather.7
  502.3 32.9 reduce-scatter.4
